TPU v7x, 128 devices: a whole 4x4x4 slice. The times are simulated.
128 devices in a mesh: section: 2 (over z_lo), patch: 4 (over y), shard: 16 (over z_hi, x, core).
Axes of the slice: x: 4, y: 4, z: 4 (z_hi: 2, z_lo: 2; z = z_hi * 2 + z_lo), core: 2. Of those that a mesh axis runs over, the one named last changes fastest.
Arguments:
- hidden: bfloat16 [32, 1024, 2432], P('shard', 'patch'), may hold values from -6 to 6
- text_kv: bfloat16 [2, 32, 154, 2432], P('section', 'shard'), may hold values from -6 to 6, as said below
- stale_kv: bfloat16 [2, 32, 1024, 2432], P('section', 'shard', 'patch'), may hold values from -6 to 6, as said below
- modulation: float32 [2, 32, 3, 2432], P('section', 'shard'), may hold values from -3 to 3
- score_gain: float32 [2, 64], P('section'), may hold values from 1.5 to 4
- qkv_weight: bfloat16 [2, 2432, 3648], P('section', 'shard'), may hold values from -0.125 to 0.125
- out_weight: bfloat16 [2, 1216, 2432], P('section', None, 'shard'), may hold values from -0.15625 to 0.15625
- final_mod: float32 [32, 2, 2432], P('shard'), may hold values from -3 to 3
- final_weight: bfloat16 [2432, 64], replicated, may hold values from -0.125 to 0.125
- latent: float32 [32, 1024, 64], P('shard', ('patch', 'section')), may hold values from -6 to 6
- step_index: int32 [32], P('shard'), may hold values from 0 to 27
Outputs:
- new_kv: bfloat16 [2, 32, 1024, 2432], P('section', 'shard', 'patch')
- latent_next: float32 [32, 1024, 64], P('shard', ('patch', 'section'))
- denoised: float32 [32, 1024, 64], P('shard', ('patch', 'section'))
Inputs may be any that keep to these rules, and one draw needn't show every extreme that they name: `text_kv`: in every row the first 1216 columns are 19 heads of 64 key features, each head with mean square one up to bfloat16 rounding. `stale_kv`: in every row the first 1216 columns are 19 heads of 64 key features, each head with mean square one up to bfloat16 rounding.
All inputs are finite; a program needn't handle non-finite values.
Results may differ from a plain program's by a relative error of at most 0.008.
Values may be sent and summed in bfloat16 or wider, within the bound.
No kernel may reach another device: no remote copies, remote signals or barrier semaphores. Data moves between devices by JAX's collectives and lax.ppermute only.
A program may use at most 192 MiB of HBM per device.

v0:
```python
import math
import jax
import jax.numpy as jnp
from jax import lax
from jax.sharding import PartitionSpec as P

HEAD = 64
NSTEPS = 28
eps_norm = 1e-06
flow_shift = 3.0


def passed_along(value, axis, steps):
    count = lax.axis_size(axis)
    first, last = (max(0, -steps), min(count, count - steps))
    return lax.ppermute(value, axis, [(source, source + steps) for source in range(first, last)])


def spread(array, axis, root):
    mine = lax.axis_index(axis) == root
    return lax.psum(jnp.where(mine, array, jnp.zeros_like(array)), axis)


def sigma_of(step):
    s = 1.0 - step.astype(jnp.float32) / NSTEPS
    return flow_shift * s / (1.0 + (flow_shift - 1.0) * s)


def modulated(xf, shift, scale):
    mean = jnp.mean(xf, -1, keepdims=True)
    cent = xf - mean
    var = jnp.mean(cent * cent, -1, keepdims=True)
    return cent * lax.rsqrt(var + eps_norm) * (1.0 + scale) + shift


def attend_one(query, keys_all, width, heads):
    count = keys_all.shape[0]
    keys = keys_all[:, :width].reshape(count, heads, HEAD)
    values = keys_all[:, width:].reshape(count, heads, HEAD)
    scores = jnp.einsum("qhe,khe->hqk", query, keys, preferred_element_type=jnp.float32)
    expo = jnp.exp(scores)
    total = jnp.sum(expo, -1)
    weights = expo.astype(jnp.bfloat16)
    mixed = jnp.einsum("hqk,khe->qhe", weights, values, preferred_element_type=jnp.float32)
    mixed = mixed / jnp.transpose(total)[:, :, None]
    return mixed.reshape(query.shape[0], width).astype(jnp.bfloat16)


def run_layer(x, stale_all, text_one, mod_one, gain, w_qkv, w_out, patch_index):
    requests, rows = (x.shape[0], x.shape[1])
    width = w_out.shape[0]
    heads = width // HEAD
    xf = x.astype(jnp.float32)
    normed = modulated(xf, mod_one[:, 0:1, :], mod_one[:, 1:2, :]).astype(jnp.bfloat16)
    proj_in = jnp.einsum("rid,dc->ric", normed, w_qkv, preferred_element_type=jnp.float32)
    q = proj_in[..., :width].reshape(requests, rows, heads, HEAD)
    k = proj_in[..., width : 2 * width].reshape(requests, rows, heads, HEAD)
    v = proj_in[..., 2 * width :]
    q_hat = q * lax.rsqrt(jnp.mean(q * q, -1, keepdims=True) + eps_norm)
    k_hat = k * lax.rsqrt(jnp.mean(k * k, -1, keepdims=True) + eps_norm)
    fresh = jnp.concatenate(
        [k_hat.reshape(requests, rows, width).astype(jnp.bfloat16), v.astype(jnp.bfloat16)], -1
    )
    query = (q_hat * gain / math.sqrt(HEAD)).astype(jnp.bfloat16)
    mixed = lax.dynamic_update_slice_in_dim(stale_all, fresh, patch_index * rows, 1)
    keys_all = jnp.concatenate([text_one, mixed], 1)

    def per_request(pair):
        return attend_one(pair[0], pair[1], width, heads)

    attn = lax.map(per_request, (query, keys_all))
    proj = jnp.einsum("riw,wd->rid", attn, w_out, preferred_element_type=jnp.float32)
    x_next = (xf + mod_one[:, 2:3, :] * proj).astype(jnp.bfloat16)
    return (x_next, fresh)


def on_device(
    hidden,
    text_kv,
    stale_kv,
    modulation,
    score_gain,
    qkv_weight,
    out_weight,
    final_mod,
    final_weight,
    latent,
    step_index,
):
    w_qkv, w_out = (
        lax.all_gather(qkv_weight[0], "shard", axis=0, tiled=True),
        lax.all_gather(out_weight[0], "shard", axis=1, tiled=True),
    )
    stale_all = lax.all_gather(stale_kv[0], "patch", axis=1, tiled=True)
    section = lax.axis_index("section")
    patch_index = lax.axis_index("patch")

    def compute(x):
        return run_layer(
            x, stale_all, text_kv[0], modulation[0], score_gain[0], w_qkv, w_out, patch_index
        )

    def passing(x):
        return (x, jnp.zeros(stale_kv.shape[1:], jnp.bfloat16))

    first, fresh_first = lax.cond(section == 0, compute, passing, hidden)
    arrived = passed_along(first, "section", 1)
    last, fresh_last = lax.cond(section == 1, compute, passing, arrived)
    fresh = jnp.where(section == 0, fresh_first, fresh_last)
    final = modulated(last.astype(jnp.float32), final_mod[:, 0:1, :], final_mod[:, 1:2, :]).astype(
        jnp.bfloat16
    )
    velocity = jnp.einsum("rid,dc->ric", final, final_weight, preferred_element_type=jnp.float32)
    half = latent.shape[1]
    shared = spread(velocity.astype(jnp.bfloat16), "section", 1).astype(velocity.dtype)
    velocity_mine = lax.dynamic_slice_in_dim(shared, section * half, half, 1)
    sig = sigma_of(step_index)[:, None, None]
    sig_next = sigma_of(step_index + 1)[:, None, None]
    latent_next = latent + (sig_next - sig) * velocity_mine
    denoised = latent - sig * velocity_mine
    return (fresh[None], latent_next, denoised)


def solution(mesh):
    in_specs = (
        P("shard", "patch", None),
        P("section", "shard", None, None),
        P("section", "shard", "patch", None),
        P("section", "shard", None, None),
        P("section", None),
        P("section", "shard", None),
        P("section", None, "shard"),
        P("shard", None, None),
        P(),
        P("shard", ("patch", "section"), None),
        P("shard"),
    )
    out_specs = (
        P("section", "shard", "patch", None),
        P("shard", ("patch", "section"), None),
        P("shard", ("patch", "section"), None),
    )
    return jax.shard_map(
        on_device, mesh=mesh, in_specs=in_specs, out_specs=out_specs, check_vma=False
    )
```

profile of v0, /device:TPU:1, one launch (start us, length us, event | category | flops | bytes accessed | tf_op | source)
XLA Modules:
  0.0 642.9 jit_solution(3232019068005679391)
XLA Ops:
  8.0 4.5 copy.28
  13.3 64.7 %all-gather.11.cloned.1.call-done = bf16[1,1216,2432]{1,2,0:T(8,128)(2,1)} async-done(((bf16[1,1216,152]{1,2,0:T(8,128)(2,1)}), bf16[1,1216,2432]{1,2,0:T(8,128)(2,1)}) %all-gather.11.cloned.1.call-update) | async-done | bytes 5914640 | tf_op jit(solution)/shard_map/all_gather | solution.py:92
  78.0 100.0 %all-gather.9.cloned.1.call-done = bf16[1,2,1024,2432]{2,3,1,0:T(8,128)(2,1)} async-done(((bf16[1,2,256,2432]{2,3,1,0:T(8,128)(2,1)}), bf16[1,2,1024,2432]{2,3,1,0:T(8,128)(2,1)}) %all-gather.9.cloned.1.call-update) | async-done | bytes 9961488 | tf_op jit(solution)/shard_map/all_gather | solution.py:94
  177.9 120.4 %all-gather.7.cloned.1.call-done = bf16[1,2432,3648]{2,1,0:T(8,128)(2,1)} async-done(((bf16[1,152,3648]{2,1,0:T(8,128)(2,1)}), bf16[1,2432,3648]{2,1,0:T(8,128)(2,1)}) %all-gather.7.cloned.1.call-update) | async-done | bytes 17743888 | tf_op jit(solution)/shard_map/all_gather | solution.py:91
  298.4 129.6 %conditional.2 = (bf16[2,256,2432]{2,1,0:T(8,128)(2,1)S(1)}, bf16[2,256,2432]{2,1,0:T(8,128)(2,1)}) conditional(s32[]{:T(128)} %convert_element_type.88, bf16[2,256,2432]{2,1,0:T(8,128)(2,1)S(1)} %copy-done.2, (bf16[2,256,2432]{2,1,0:T(8,128)(2,1)S(1)}, f32[1,2,3,2432]{3,1,2,0:T(2,128)S(1)}, bf16[2432,3648]{1,0:T(8,128)(2,1)}, f32[1,64]{1,0:T(1,128)S(1)}, ...), branch_computations={%region_0.0_spmd, %region_1.9_spmd} | conditional | flops 13646128128 | bytes 220811024 | solution.py:106
  300.2 16.5 %fusion.6 = f32[2,256,3648]{1,2,0:T(8,128)} fusion(bf16[2432,3648]{1,0:T(8,128)(2,1)} %get-tuple-element.139, bf16[2,256,2432]{2,1,0:T(8,128)(2,1)S(1)} %get-tuple-element.71, f32[2,2432]{1,0:T(2,128)S(1)} %get-tuple-element.182, f32[2,2432]{1,0:T(2,128)S(1)} %get-tuple-element.183, f32[2,256]{1,0:T(2,128)S(1)} %add_rsqrt_fusion.2, ...), kind=kOutput, calls=%fused_computation.11 | convolution fusion | flops 9092333568 | bytes 27748352 | tf_op jit(solution)/shard_map/cond/branch_1_fun/rid,dc->ric/dot_general | solution.py:55
  316.7 3.3 slice_multiply_fusion
  320.1 2.0 reduce_sum.99
  322.1 4.7 fusion.76
  326.7 2.9 slice.91
  329.6 8.8 %copy.62 = bf16[2,1024,2432]{1,2,0:T(8,128)(2,1)} copy(bf16[2,1024,2432]{1,2,0:T(8,128)(2,1)} %get-tuple-element.74) | data formatting | bytes 19922944 | tf_op jit(solution)/shard_map/cond
  338.4 4.3 pad_maximum_fusion.1
  342.7 5.8 copy.30
  348.5 13.1 %pad_maximum_fusion = bf16[2,1178,2432]{1,2,0:T(8,128)(2,1)} fusion(bf16[2,1024,2432]{1,2,0:T(8,128)(2,1)} %get-tuple-element.180, bf16[2,154,2432]{1,2,0:T(8,128)(2,1)} %bitcast.147), kind=kLoop, calls=%fused_computation.13 | loop fusion | flops 22919168 | bytes 22919168 | tf_op jit(solution)/shard_map/cond/branch_1_fun/concatenate | solution.py:66
  361.9 1.5 multiply_convert_fusion
  363.5 52.4 %while.18 = (s32[]{:T(128)}, bf16[2,256,1216]{1,2,0:T(8,128)(2,1)}, bf16[2,1178,2432]{1,2,0:T(8,128)(2,1)}, bf16[2,256,19,64]{1,3,2,0:T(8,128)(2,1)}, s32[]{:T(128)}) while((s32[]{:T(128)}, bf16[2,256,1216]{1,2,0:T(8,128)(2,1)}, bf16[2,1178,2432]{1,2,0:T(8,128)(2,1)}, bf16[2,256,19,64]{1,3,2,0:T(8,128)(2,1)}, s32[]{:T(128)}) %tuple.88), condition=%wide.region_8.8_spmd, body=%wide.region_6.7_spmd.sunk | while | flops 1478904064 | bytes 82245984 | solution.py:71
  364.0 3.2 dynamic-slice_bitcast_fusion.5
  368.4 9.7 %exponential_reduce_fusion.5 = (f32[19,256]{1,0:T(8,128)S(1)}, f32[19,256,1178]{1,2,0:T(8,128)}) fusion(bf16[1178,19,64]{0,2,1:T(8,128)(2,1)S(1)} %bitcast.134, bf16[2,256,19,64]{1,3,2,0:T(8,128)(2,1)S(1)} %copy-done.5, s32[]{:T(128)} %get-tuple-element.287), kind=kOutput, calls=%fused_computation.clone.1 | convolution fusion | flops 739138304 | bytes 26674180 | tf_op jit(solution)/shard_map/cond/branch_1_fun/while/body/eval_jaxpr/qhe,khe->hqk/dot_general | solution.py:40
  378.1 10.9 %divide_convert_fusion.5 = bf16[256,19,64]{0,2,1:T(8,128)(2,1)S(1)} fusion(bf16[1178,19,64]{0,2,1:T(8,128)(2,1)S(1)} %bitcast.136, f32[19,256,1178]{1,2,0:T(8,128)} %get-tuple-element.265, f32[256,19]{0,1:T(8,128)S(1)} %bitcast.150), kind=kOutput, calls=%fused_computation.5.clone.1 | convolution fusion | flops 739765760 | bytes 26426112 | tf_op jit(solution)/shard_map/cond/branch_1_fun/while/body/eval_jaxpr/hqk,khe->qhe/dot_general | solution.py:44
  389.9 3.2 dynamic-slice_bitcast_fusion.5
  394.4 9.7 %exponential_reduce_fusion.5 = (f32[19,256]{1,0:T(8,128)S(1)}, f32[19,256,1178]{1,2,0:T(8,128)}) fusion(bf16[1178,19,64]{0,2,1:T(8,128)(2,1)S(1)} %bitcast.134, bf16[2,256,19,64]{1,3,2,0:T(8,128)(2,1)S(1)} %copy-done.5, s32[]{:T(128)} %get-tuple-element.287), kind=kOutput, calls=%fused_computation.clone.1 | convolution fusion | flops 739138304 | bytes 26674180 | tf_op jit(solution)/shard_map/cond/branch_1_fun/while/body/eval_jaxpr/qhe,khe->hqk/dot_general | solution.py:40
  404.1 10.9 %divide_convert_fusion.5 = bf16[256,19,64]{0,2,1:T(8,128)(2,1)S(1)} fusion(bf16[1178,19,64]{0,2,1:T(8,128)(2,1)S(1)} %bitcast.136, f32[19,256,1178]{1,2,0:T(8,128)} %get-tuple-element.265, f32[256,19]{0,1:T(8,128)S(1)} %bitcast.150), kind=kOutput, calls=%fused_computation.5.clone.1 | convolution fusion | flops 739765760 | bytes 26426112 | tf_op jit(solution)/shard_map/cond/branch_1_fun/while/body/eval_jaxpr/hqk,khe->qhe/dot_general | solution.py:44
  415.9 7.6 %fusion.19 = bf16[2,256,2432]{2,1,0:T(8,128)(2,1)S(1)} fusion(bf16[2,256,2432]{2,1,0:T(8,128)(2,1)S(1)} %get-tuple-element.71, bf16[2,256,1216]{1,2,0:T(8,128)(2,1)} %get-tuple-element.78, bf16[1216,2432]{0,1:T(8,128)(2,1)} %get-tuple-element.144, f32[2,2432]{1,0:T(2,128)S(1)} %copy-done.10), kind=kOutput, calls=%fused_computation.26 | convolution fusion | flops 3033268224 | bytes 12160000 | tf_op jit(solution)/shard_map/cond/branch_1_fun/riw,wd->rid/dot_general | solution.py:72
  423.5 4.3 copy.46
  428.0 1.5 copy-done.1
  432.2 52.4 %collective-permute-done = bf16[2,256,2432]{2,1,0:T(8,128)(2,1)S(1)} collective-permute-done((bf16[2,256,2432]{2,1,0:T(8,128)(2,1)}, bf16[2,256,2432]{2,1,0:T(8,128)(2,1)S(1)}, u32[]{:S(2)}, u32[]{:S(2)}) %collective-permute-start) | collective-permute-done | bytes 2490400 | tf_op jit(solution)/shard_map/ppermute | solution.py:16
  484.6 4.3 conditional.3
  484.6 1.6 broadcast.161.clone
  490.2 1.8 fusion.69
  492.0 3.4 select_bitcast_fusion
  495.5 138.9 %all-reduce.2.cloned.1.call-done = bf16[2,256,64]{1,2,0:T(8,128)(2,1)} async-done(((bf16[2,256,64]{1,2,0:T(8,128)(2,1)}), bf16[2,256,64]{1,2,0:T(8,128)(2,1)}) %all-reduce.2.cloned.1.call-update) | async-done | bytes 65552 | tf_op jit(solution)/shard_map/psum | solution.py:21
  634.4 1.5 fusion.73
  (60 shorter events, 12.0 us)
Async XLA Ops:
  7.2 483.0 %copy-start = (bf16[2432,64]{0,1:T(8,128)(2,1)S(1)}, bf16[2432,64]{0,1:T(8,128)(2,1)}, u32[]{:S(2)}) copy-start(bf16[2432,64]{0,1:T(8,128)(2,1)} %param.27) | copy-start | bytes 933892
  7.2 70.8 %all-gather.11.cloned.1.call-start = ((), (), s32[]{:S(2)}) async-start(), calls=%async_computation.3 | async-start | bytes 6615040 | tf_op jit(solution)/shard_map/all_gather | solution.py:92
  7.9 290.4 %copy-start.2 = (bf16[2,256,2432]{2,1,0:T(8,128)(2,1)S(1)}, bf16[2,256,2432]{2,1,0:T(8,128)(2,1)}, u32[]{:S(2)}) copy-start(bf16[2,256,2432]{2,1,0:T(8,128)(2,1)} %param.19) | copy-start | bytes 7471108
  7.9 290.4 %copy-start.7 = (f32[1,2,3,2432]{3,1,2,0:T(2,128)S(1)}, f32[1,2,3,2432]{3,1,2,0:T(2,128)}, u32[]{:S(2)}) copy-start(f32[1,2,3,2432]{3,1,2,0:T(2,128)} %param.22) | copy-start | bytes 175108
  7.9 290.4 %copy-start.14 = (f32[1,64]{1,0:T(1,128)S(1)}, f32[1,64]{1,0:T(1,128)}, u32[]{:S(2)}) copy-start(f32[1,64]{1,0:T(1,128)} %param.23) | copy-start | bytes 772
  7.9 170.0 %all-gather.9.cloned.1.call-start = ((), (), s32[]{:S(2)}) async-start(), calls=%async_computation.2 | async-start | bytes 12451840 | tf_op jit(solution)/shard_map/all_gather | solution.py:94
  12.5 285.9 %all-gather.7.cloned.1.call-start = ((), (), s32[]{:S(2)}) async-start(), calls=%async_computation.1 | async-start | bytes 19183616 | tf_op jit(solution)/shard_map/all_gather | solution.py:91
  13.2 621.2 %all-reduce.2.cloned.1.call-start = ((), (), s32[]{:S(2)}) async-start(), calls=%async_computation | async-start | bytes 131072 | tf_op jit(solution)/shard_map/psum | solution.py:21
  298.4 132.5 %copy-start.17 = (s32[2]{0:T(128)S(1)}, s32[2]{0:T(128)}, u32[]{:S(2)}) copy-start(s32[2]{0:T(128)} %param.29) | copy-start | bytes 28
  298.4 133.1 %copy-start.9 = (f32[2,2,2432]{2,1,0:T(2,128)S(1)}, f32[2,2,2432]{2,1,0:T(2,128)}, u32[]{:S(2)}) copy-start(f32[2,2,2432]{2,1,0:T(2,128)} %param.26) | copy-start | bytes 116740
  348.5 13.1 %copy-start.3 = (f32[2,256,1216]{1,2,0:T(8,128)S(1)}, f32[2,256,1216]{1,2,0:T(8,128)}, u32[]{:S(2)}) copy-start(f32[2,256,1216]{1,2,0:T(8,128)} %get-tuple-element.177) | copy-start | bytes 7471108 | tf_op jit(solution)/shard_map/cond
  363.5 52.4 %copy-start.10 = (f32[2,2432]{1,0:T(2,128)S(1)}, f32[2,2432]{1,0:T(2,128)}, u32[]{:S(2)}) copy-start(f32[2,2432]{1,0:T(2,128)} %get-tuple-element.181) | copy-start | bytes 58372 | tf_op jit(solution)/shard_map/cond
  367.1 1.3 copy-start.5
  393.1 1.3 copy-start.5
  428.0 1.5 copy-start.1
  429.4 55.1 %collective-permute-start = (bf16[2,256,2432]{2,1,0:T(8,128)(2,1)}, bf16[2,256,2432]{2,1,0:T(8,128)(2,1)S(1)}, u32[]{:S(2)}, u32[]{:S(2)}) collective-permute-start(bf16[2,256,2432]{2,1,0:T(8,128)(2,1)} %copy-done.1), channel_id=1, source_target_pairs={{0,64},{1,65},{2,66},{3,67},{4,68},{5,69},{6,70},{7,71},{8,72},{9,... | collective-permute-start | bytes 7471112 | tf_op jit(solution)/shard_map/ppermute | solution.py:16
  488.9 1.2 copy-start.12
  488.9 1.2 copy-start.13
  492.0 142.4 %copy-start.8 = (f32[2,128,64]{1,2,0:T(8,128)S(1)}, f32[2,128,64]{1,2,0:T(8,128)}, u32[]{:S(2)}) copy-start(f32[2,128,64]{1,2,0:T(8,128)} %param.28) | copy-start | bytes 196612
  492.0 142.4 %copy-start.15 = (f32[2]{0:T(128)S(1)}, f32[2]{0:T(128)}, u32[]{:S(2)}) copy-start(f32[2]{0:T(128)} %get-tuple-element.171) | copy-start | bytes 28
  492.0 142.4 %copy-start.16 = (f32[2]{0:T(128)S(1)}, f32[2]{0:T(128)}, u32[]{:S(2)}) copy-start(f32[2]{0:T(128)} %get-tuple-element.172) | copy-start | bytes 28
Sparse Core Ops, SparseCore 0:
  10.4 67.5 all-gather.10
  80.2 97.6 all-gather.8
  180.5 117.8 all-gather.6
  492.1 142.2 all-reduce.1
where the time goes:
time: 652 us; the launch traced here: 643 us
  waiting for transfers between devices  478 us (73%)
  matrix products  67.2 us (10%)
  local copies, waits for them, and re-layouts  40.7 us (6%)
  other arithmetic  37.8 us (6%)
  between operations  14.4 us (2%)
    psum x1, waiting for transfers between devices, spread(): return lax.psum(jnp.where(mine, array, jnp.zeros_like(array)), axis)  139 us
    all_gather x1, waiting for transfers between devices, on_device(): lax.all_gather(qkv_weight[0], 'shard', axis=0, tiled=True)  120 us
    all_gather x1, waiting for transfers between devices, on_device(): stale_all = lax.all_gather(stale_kv[0], 'patch', axis=1, tiled=True)  100 us
    all_gather x1, waiting for transfers between devices, on_device(): lax.all_gather(out_weight[0], 'shard', axis=1, tiled=True)  64.7 us
    ppermute x1, waiting for transfers between devices, passed_along(): lax.ppermute(value, axis, [(source, source + steps) for source in range(f...  52.4 us
    dot_general x2, matrix products, attend_one(): jnp.einsum('hqk,khe->qhe', weights, values, preferred_element_type=jnp.fl...  21.8 us
    dot_general x2, matrix products, attend_one(): jnp.einsum('qhe,khe->hqk', query, keys, preferred_element_type=jnp.float32)  19.4 us
    dot_general x1, matrix products, run_layer(): jnp.einsum('rid,dc->ric', normed, w_qkv, preferred_element_type=jnp.float32)  16.5 us
  transfers between devices with their start and end apart: 5, of which 5 were waited for; matrix products, arithmetic and copies ran while one was open for 1% of the time, Pallas kernels for 0%

commit v1 on v0

--- a/solution.py
+++ b/solution.py
@@ -18,7 +18,7 @@
 
 def spread(array, axis, root):
     mine = lax.axis_index(axis) == root
-    return lax.psum(jnp.where(mine, array, jnp.zeros_like(array)), axis)
+    return jnp.sum(lax.all_gather(jnp.where(mine, array, jnp.zeros_like(array)), axis), axis=0)
 
 
 def sigma_of(step):

time: 652 us -> 633 us (0.971)
  waiting for transfers between devices: 478 us -> 339 us
  blocking collectives: 0 us -> 120 us
    psum x1 -> x0, waiting for transfers between devices: 139 us -> none  [spread(): return lax.psum(jnp.where(mine, array, jnp.zeros_like(array)), axis)]
    all_gather x0 -> x1, blocking collectives: none -> 120 us  [spread(): lax.all_gather(jnp.where(mine, array, jnp.zeros_like(array)), axis)]
  transfers between devices with their start and end apart: 5 -> 4, of which waited for: 5 -> 4; matrix products, arithmetic and copies ran while one was open for 1% -> 1% of each run, Pallas kernels for 0% -> 0%
where the time goes in v1:
time: 633 us; the launch traced here: 623 us
  waiting for transfers between devices  339 us (54%)
  blocking collectives  120 us (19%)
  matrix products  66.5 us (11%)
  local copies, waits for them, and re-layouts  40.6 us (6%)
  other arithmetic  37.1 us (6%)
  between operations  14.4 us (2%)
    all_gather x1, blocking collectives, spread(): lax.all_gather(jnp.where(mine, array, jnp.zeros_like(array)), axis)  120 us
    all_gather x1, waiting for transfers between devices, on_device(): lax.all_gather(qkv_weight[0], 'shard', axis=0, tiled=True)  120 us
    all_gather x1, waiting for transfers between devices, on_device(): stale_all = lax.all_gather(stale_kv[0], 'patch', axis=1, tiled=True)  100 us
    all_gather x1, waiting for transfers between devices, on_device(): lax.all_gather(out_weight[0], 'shard', axis=1, tiled=True)  64.7 us
    ppermute x1, waiting for transfers between devices, passed_along(): lax.ppermute(value, axis, [(source, source + steps) for source in range(f...  52.4 us
    dot_general x2, matrix products, attend_one(): jnp.einsum('hqk,khe->qhe', weights, values, preferred_element_type=jnp.fl...  21.8 us
    dot_general x2, matrix products, attend_one(): jnp.einsum('qhe,khe->hqk', query, keys, preferred_element_type=jnp.float32)  19.3 us
    dot_general x1, matrix products, run_layer(): jnp.einsum('rid,dc->ric', normed, w_qkv, preferred_element_type=jnp.float32)  16.5 us
  transfers between devices with their start and end apart: 4, of which 4 were waited for; matrix products, arithmetic and copies ran while one was open for 1% of the time, Pallas kernels for 0%

profile of v1, /device:TPU:1, one launch (start us, length us, event | category | flops | bytes accessed | tf_op | source)
XLA Modules:
  0.0 623.0 jit_solution(69874999075712283)
XLA Ops:
  8.0 4.5 copy.28
  13.2 64.7 %all-gather.12.cloned.1.call-done = bf16[1,1216,2432]{1,2,0:T(8,128)(2,1)} async-done(((bf16[1,1216,152]{1,2,0:T(8,128)(2,1)}), bf16[1,1216,2432]{1,2,0:T(8,128)(2,1)}) %all-gather.12.cloned.1.call-update) | async-done | bytes 5914640 | tf_op jit(solution)/shard_map/all_gather | solution.py:92
  78.0 100.0 %all-gather.10.cloned.1.call-done = bf16[1,2,1024,2432]{2,3,1,0:T(8,128)(2,1)} async-done(((bf16[1,2,256,2432]{2,3,1,0:T(8,128)(2,1)}), bf16[1,2,1024,2432]{2,3,1,0:T(8,128)(2,1)}) %all-gather.10.cloned.1.call-update) | async-done | bytes 9961488 | tf_op jit(solution)/shard_map/all_gather | solution.py:94
  177.9 120.4 %all-gather.8.cloned.1.call-done = bf16[1,2432,3648]{2,1,0:T(8,128)(2,1)} async-done(((bf16[1,152,3648]{2,1,0:T(8,128)(2,1)}), bf16[1,2432,3648]{2,1,0:T(8,128)(2,1)}) %all-gather.8.cloned.1.call-update) | async-done | bytes 17743888 | tf_op jit(solution)/shard_map/all_gather | solution.py:91
  298.4 129.6 %conditional.2 = (bf16[2,256,2432]{2,1,0:T(8,128)(2,1)S(1)}, bf16[2,256,2432]{2,1,0:T(8,128)(2,1)}) conditional(s32[]{:T(128)} %convert_element_type.90, bf16[2,256,2432]{2,1,0:T(8,128)(2,1)S(1)} %copy-done.2, (bf16[2,256,2432]{2,1,0:T(8,128)(2,1)S(1)}, f32[1,2,3,2432]{3,1,2,0:T(2,128)S(1)}, bf16[2432,3648]{1,0:T(8,128)(2,1)}, f32[1,64]{1,0:T(1,128)S(1)}, ...), branch_computations={%region_0.0_spmd, %region_1.9_spmd} | conditional | flops 13646128128 | bytes 220811024 | solution.py:106
  300.2 16.5 %fusion.6 = f32[2,256,3648]{1,2,0:T(8,128)} fusion(bf16[2432,3648]{1,0:T(8,128)(2,1)} %get-tuple-element.139, bf16[2,256,2432]{2,1,0:T(8,128)(2,1)S(1)} %get-tuple-element.71, f32[2,2432]{1,0:T(2,128)S(1)} %get-tuple-element.182, f32[2,2432]{1,0:T(2,128)S(1)} %get-tuple-element.183, f32[2,256]{1,0:T(2,128)S(1)} %add_rsqrt_fusion.2, ...), kind=kOutput, calls=%fused_computation.11 | convolution fusion | flops 9092333568 | bytes 27748352 | tf_op jit(solution)/shard_map/cond/branch_1_fun/rid,dc->ric/dot_general | solution.py:55
  316.7 3.3 slice_multiply_fusion
  320.1 2.0 reduce_sum.110
  322.0 4.6 fusion.76
  326.7 2.9 slice.91
  329.6 8.8 %copy.62 = bf16[2,1024,2432]{1,2,0:T(8,128)(2,1)} copy(bf16[2,1024,2432]{1,2,0:T(8,128)(2,1)} %get-tuple-element.74) | data formatting | bytes 19922944 | tf_op jit(solution)/shard_map/cond
  338.4 4.3 pad_maximum_fusion.1
  342.7 5.8 copy.30
  348.5 13.1 %pad_maximum_fusion = bf16[2,1178,2432]{1,2,0:T(8,128)(2,1)} fusion(bf16[2,1024,2432]{1,2,0:T(8,128)(2,1)} %get-tuple-element.180, bf16[2,154,2432]{1,2,0:T(8,128)(2,1)} %bitcast.148), kind=kLoop, calls=%fused_computation.13 | loop fusion | flops 22919168 | bytes 22919168 | tf_op jit(solution)/shard_map/cond/branch_1_fun/concatenate | solution.py:66
  361.9 1.5 multiply_convert_fusion
  363.4 52.4 %while.18 = (s32[]{:T(128)}, bf16[2,256,1216]{1,2,0:T(8,128)(2,1)}, bf16[2,1178,2432]{1,2,0:T(8,128)(2,1)}, bf16[2,256,19,64]{1,3,2,0:T(8,128)(2,1)}, s32[]{:T(128)}) while((s32[]{:T(128)}, bf16[2,256,1216]{1,2,0:T(8,128)(2,1)}, bf16[2,1178,2432]{1,2,0:T(8,128)(2,1)}, bf16[2,256,19,64]{1,3,2,0:T(8,128)(2,1)}, s32[]{:T(128)}) %tuple.88), condition=%wide.region_8.8_spmd, body=%wide.region_6.7_spmd.sunk | while | flops 1478904064 | bytes 82245984 | solution.py:71
  363.9 3.2 dynamic-slice_bitcast_fusion.5
  368.4 9.7 %exponential_reduce_fusion.5 = (f32[19,256]{1,0:T(8,128)S(1)}, f32[19,256,1178]{1,2,0:T(8,128)}) fusion(bf16[1178,19,64]{0,2,1:T(8,128)(2,1)S(1)} %bitcast.135, bf16[2,256,19,64]{1,3,2,0:T(8,128)(2,1)S(1)} %copy-done.5, s32[]{:T(128)} %get-tuple-element.287), kind=kOutput, calls=%fused_computation.clone.1 | convolution fusion | flops 739138304 | bytes 26674180 | tf_op jit(solution)/shard_map/cond/branch_1_fun/while/body/eval_jaxpr/qhe,khe->hqk/dot_general | solution.py:40
  378.1 10.9 %divide_convert_fusion.5 = bf16[256,19,64]{0,2,1:T(8,128)(2,1)S(1)} fusion(bf16[1178,19,64]{0,2,1:T(8,128)(2,1)S(1)} %bitcast.137, f32[19,256,1178]{1,2,0:T(8,128)} %get-tuple-element.265, f32[256,19]{0,1:T(8,128)S(1)} %bitcast.151), kind=kOutput, calls=%fused_computation.5.clone.1 | convolution fusion | flops 739765760 | bytes 26426112 | tf_op jit(solution)/shard_map/cond/branch_1_fun/while/body/eval_jaxpr/hqk,khe->qhe/dot_general | solution.py:44
  389.9 3.2 dynamic-slice_bitcast_fusion.5
  394.3 9.7 %exponential_reduce_fusion.5 = (f32[19,256]{1,0:T(8,128)S(1)}, f32[19,256,1178]{1,2,0:T(8,128)}) fusion(bf16[1178,19,64]{0,2,1:T(8,128)(2,1)S(1)} %bitcast.135, bf16[2,256,19,64]{1,3,2,0:T(8,128)(2,1)S(1)} %copy-done.5, s32[]{:T(128)} %get-tuple-element.287), kind=kOutput, calls=%fused_computation.clone.1 | convolution fusion | flops 739138304 | bytes 26674180 | tf_op jit(solution)/shard_map/cond/branch_1_fun/while/body/eval_jaxpr/qhe,khe->hqk/dot_general | solution.py:40
  404.0 10.9 %divide_convert_fusion.5 = bf16[256,19,64]{0,2,1:T(8,128)(2,1)S(1)} fusion(bf16[1178,19,64]{0,2,1:T(8,128)(2,1)S(1)} %bitcast.137, f32[19,256,1178]{1,2,0:T(8,128)} %get-tuple-element.265, f32[256,19]{0,1:T(8,128)S(1)} %bitcast.151), kind=kOutput, calls=%fused_computation.5.clone.1 | convolution fusion | flops 739765760 | bytes 26426112 | tf_op jit(solution)/shard_map/cond/branch_1_fun/while/body/eval_jaxpr/hqk,khe->qhe/dot_general | solution.py:44
  415.8 7.6 %fusion.19 = bf16[2,256,2432]{2,1,0:T(8,128)(2,1)S(1)} fusion(bf16[2,256,2432]{2,1,0:T(8,128)(2,1)S(1)} %get-tuple-element.71, bf16[2,256,1216]{1,2,0:T(8,128)(2,1)} %get-tuple-element.78, bf16[1216,2432]{0,1:T(8,128)(2,1)} %get-tuple-element.144, f32[2,2432]{1,0:T(2,128)S(1)} %copy-done.10), kind=kOutput, calls=%fused_computation.26 | convolution fusion | flops 3033268224 | bytes 12160000 | tf_op jit(solution)/shard_map/cond/branch_1_fun/riw,wd->rid/dot_general | solution.py:72
  423.4 4.3 copy.46
  427.9 1.4 copy-done.1
  429.4 1.4 collective-permute-start
  432.1 52.4 %collective-permute-done = bf16[2,256,2432]{2,1,0:T(8,128)(2,1)S(1)} collective-permute-done((bf16[2,256,2432]{2,1,0:T(8,128)(2,1)}, bf16[2,256,2432]{2,1,0:T(8,128)(2,1)S(1)}, u32[]{:S(2)}, u32[]{:S(2)}) %collective-permute-start) | collective-permute-done | bytes 2490400 | tf_op jit(solution)/shard_map/ppermute | solution.py:16
  484.5 4.3 conditional.3
  484.5 1.6 broadcast.161.clone
  490.1 1.2 fusion.69
  491.3 120.5 %all-gather.3 = bf16[4,256,64]{1,2,0:T(8,128)(2,1)S(1)} all-gather(bf16[2,256,64]{1,2,0:T(8,128)(2,1)S(1)} %fusion.69), channel_id=5, replica_groups=mesh['section'=2,'patch'=4,'shard'=16] {'section'}, dimensions={0}, use_global_device_ids=true | all-gather | bytes 196608 | tf_op jit(solution)/shard_map/all_gather | solution.py:21
  611.9 3.4 select_bitcast_fusion
  (59 shorter events, 11.2 us)
Async XLA Ops:
  7.2 482.9 %copy-start = (bf16[2432,64]{0,1:T(8,128)(2,1)S(1)}, bf16[2432,64]{0,1:T(8,128)(2,1)}, u32[]{:S(2)}) copy-start(bf16[2432,64]{0,1:T(8,128)(2,1)} %param.27) | copy-start | bytes 933892
  7.2 70.8 %all-gather.12.cloned.1.call-start = ((), (), s32[]{:S(2)}) async-start(), calls=%async_computation.2 | async-start | bytes 6615040 | tf_op jit(solution)/shard_map/all_gather | solution.py:92
  7.9 290.4 %copy-start.2 = (bf16[2,256,2432]{2,1,0:T(8,128)(2,1)S(1)}, bf16[2,256,2432]{2,1,0:T(8,128)(2,1)}, u32[]{:S(2)}) copy-start(bf16[2,256,2432]{2,1,0:T(8,128)(2,1)} %param.19) | copy-start | bytes 7471108
  7.9 290.4 %copy-start.7 = (f32[1,2,3,2432]{3,1,2,0:T(2,128)S(1)}, f32[1,2,3,2432]{3,1,2,0:T(2,128)}, u32[]{:S(2)}) copy-start(f32[1,2,3,2432]{3,1,2,0:T(2,128)} %param.22) | copy-start | bytes 175108
  7.9 290.4 %copy-start.14 = (f32[1,64]{1,0:T(1,128)S(1)}, f32[1,64]{1,0:T(1,128)}, u32[]{:S(2)}) copy-start(f32[1,64]{1,0:T(1,128)} %param.23) | copy-start | bytes 772
  7.9 170.0 %all-gather.10.cloned.1.call-start = ((), (), s32[]{:S(2)}) async-start(), calls=%async_computation.1 | async-start | bytes 12451840 | tf_op jit(solution)/shard_map/all_gather | solution.py:94
  12.5 285.9 %all-gather.8.cloned.1.call-start = ((), (), s32[]{:S(2)}) async-start(), calls=%async_computation | async-start | bytes 19183616 | tf_op jit(solution)/shard_map/all_gather | solution.py:91
  298.4 132.5 %copy-start.17 = (s32[2]{0:T(128)S(1)}, s32[2]{0:T(128)}, u32[]{:S(2)}) copy-start(s32[2]{0:T(128)} %param.29) | copy-start | bytes 28
  298.4 133.1 %copy-start.9 = (f32[2,2,2432]{2,1,0:T(2,128)S(1)}, f32[2,2,2432]{2,1,0:T(2,128)}, u32[]{:S(2)}) copy-start(f32[2,2,2432]{2,1,0:T(2,128)} %param.26) | copy-start | bytes 116740
  348.4 13.1 %copy-start.3 = (f32[2,256,1216]{1,2,0:T(8,128)S(1)}, f32[2,256,1216]{1,2,0:T(8,128)}, u32[]{:S(2)}) copy-start(f32[2,256,1216]{1,2,0:T(8,128)} %get-tuple-element.177) | copy-start | bytes 7471108 | tf_op jit(solution)/shard_map/cond
  363.4 52.4 %copy-start.10 = (f32[2,2432]{1,0:T(2,128)S(1)}, f32[2,2432]{1,0:T(2,128)}, u32[]{:S(2)}) copy-start(f32[2,2432]{1,0:T(2,128)} %get-tuple-element.181) | copy-start | bytes 58372 | tf_op jit(solution)/shard_map/cond
  367.1 1.3 copy-start.5
  393.0 1.3 copy-start.5
  427.9 1.5 copy-start.1
  429.4 55.1 %collective-permute-start = (bf16[2,256,2432]{2,1,0:T(8,128)(2,1)}, bf16[2,256,2432]{2,1,0:T(8,128)(2,1)S(1)}, u32[]{:S(2)}, u32[]{:S(2)}) collective-permute-start(bf16[2,256,2432]{2,1,0:T(8,128)(2,1)} %copy-done.1), channel_id=1, source_target_pairs={{0,64},{1,65},{2,66},{3,67},{4,68},{5,69},{6,70},{7,71},{8,72},{9,... | collective-permute-start | bytes 7471112 | tf_op jit(solution)/shard_map/ppermute | solution.py:16
  488.9 1.2 copy-start.12
  488.9 1.2 copy-start.13
  611.8 3.5 copy-start.8
  611.8 3.4 copy-start.15
  611.8 3.4 copy-start.16
Sparse Core Ops, SparseCore 0:
  10.4 67.5 all-gather.11
  80.2 97.6 all-gather.9
  180.5 117.8 all-gather.7
